TPU v7x, 256 devices: a whole 4x4x8 slice. The times are simulated.
256 devices in a mesh: dp: 64 (over x, z, core), mp: 4 (over y).
Axes of the slice: x: 4, y: 4, z: 8, core: 2. Of those that a mesh axis runs over, the one named last changes fastest.
Arguments:
- history: bfloat16 [1024, 32, 1024], P('dp', None, 'mp'), may hold values from -6 to 6
- lengths: int32 [1024], replicated, may hold values from 1 to 32, 16384 in all
- source: int32 [1024], replicated, may hold values from 0 to 1023, as said below
- owners: int32 [32768, 8], P(('dp', 'mp')), may hold values from 0 to 255, all different within a row; in each aligned block of 128 rows (0 to 127, 128 to 255, ...) at most 6 rows name the same one
- item_rows: int32 [32768, 8], P(('dp', 'mp')), may hold values from 0 to 511
- catalogue: bfloat16 [131072, 1024], P(('dp', 'mp')), may hold values from -6 to 6
- w_in: bfloat16 [4, 1024, 1024], P(None, None, 'mp'), may hold values from -0.1875 to 0.1875
- w_out: bfloat16 [1024, 1024], P('mp'), may hold values from -0.1875 to 0.1875
Outputs:
- w_in_grad: float32 [4, 1024, 1024], P(None, 'dp', 'mp')
- w_out_grad: float32 [1024, 1024], P('mp', 'dp')
- cat_grad: float32 [131072, 1024], P(('dp', 'mp'))
Inputs may be any that keep to these rules, and one draw needn't show every extreme that they name: `source`: a permutation; balanced slot k lies on index k // 16 of dp, and the 16 histories that start on one index of dp go to one index of dp at most (16 + 64 - 1) // 64 at a time, that many for some index. Each event names 8 different owners, column 0 the positive item's; the events of one device (aligned blocks of 128) name one owner at most 6 times.
All inputs are finite; a program needn't handle non-finite values.
Results may differ from a plain program's by a relative error of at most 0.017.
Values may be sent and summed in bfloat16 or wider, within the bound.
A program may use at most 128 MiB of HBM per device.

v0:
```python
import jax
import jax.numpy as jnp
from jax import lax
from jax.sharding import PartitionSpec as P

DH = 128
cosine_divisor = 0.05
epsilon_norm = 1e-05
epsilon_unit = 1e-06


def normalize(rows_in):
    centered = rows_in - jnp.mean(rows_in, axis=-1, keepdims=True)
    spread = jnp.mean(centered * centered, axis=-1, keepdims=True)
    return centered / jnp.sqrt(spread + epsilon_norm)


def attend(projected, length_here):
    gating = projected[0]
    values = projected[1]
    queries = projected[2]
    key_rows = projected[3]
    steps_n = projected.shape[1]
    scores = jnp.einsum(
        "thd,shd->hts", queries, key_rows, preferred_element_type=jnp.float32
    ) / jnp.sqrt(jnp.float32(projected.shape[3]))
    places = jnp.arange(steps_n, dtype=jnp.int32)
    allowed = (places[None, :] <= places[:, None]) & (places[None, :] < length_here)
    weights = jnp.where(
        allowed[None], jax.nn.silu(scores) / length_here.astype(jnp.float32), 0.0
    ).astype(jnp.bfloat16)
    mixed_out = jnp.einsum("hts,shd->thd", weights, values, preferred_element_type=jnp.float32)
    return (normalize(mixed_out) * gating.astype(jnp.float32)).astype(jnp.bfloat16)


def loss_block(out_rows, valid_rows, fetched):
    out_norm = jnp.sqrt(jnp.sum(out_rows * out_rows, axis=-1, keepdims=True) + epsilon_unit)
    request_unit_vector = out_rows / out_norm
    item_f = fetched.astype(jnp.float32)
    item_norm = jnp.sqrt(jnp.sum(item_f * item_f, axis=-1, keepdims=True) + epsilon_unit)
    catalog_unit_vector = item_f / item_norm
    cosine_match_raw = (
        jnp.einsum("qn,qgn->qg", request_unit_vector, catalog_unit_vector) / cosine_divisor
    )
    expo = jnp.exp(cosine_match_raw)
    probs = expo / jnp.sum(expo, axis=-1, keepdims=True)
    column = jnp.arange(cosine_match_raw.shape[1], dtype=jnp.int32)
    exponent_shares = (probs - (column[None, :] == 0).astype(jnp.float32)) * valid_rows[
        :, None
    ].astype(jnp.float32)
    request_unit_vector_slope = (
        jnp.einsum("as,asy->ay", exponent_shares, catalog_unit_vector) / cosine_divisor
    )
    out_grad = (
        request_unit_vector_slope
        - request_unit_vector
        * jnp.sum(request_unit_vector * request_unit_vector_slope, axis=-1, keepdims=True)
    ) / out_norm
    catalog_unit_vector_slope = (
        exponent_shares[:, :, None] * request_unit_vector[:, None, :] / cosine_divisor
    )
    item_grad = (
        catalog_unit_vector_slope
        - catalog_unit_vector
        * jnp.sum(catalog_unit_vector * catalog_unit_vector_slope, axis=-1, keepdims=True)
    ) / item_norm
    return (out_grad, item_grad)


def silu_slope(preact):
    sigma = jax.nn.sigmoid(preact)
    return sigma * (1.0 + preact * (1.0 - sigma))


def earlier_same(labels):
    order_ids = jnp.arange(labels.shape[0], dtype=jnp.int32)
    same = (labels[None, :] == labels[:, None]) & (order_ids[None, :] < order_ids[:, None])
    return jnp.sum(same.astype(jnp.int32), axis=1)


def per_device(history, lengths, source, owners, item_rows, catalogue, w_in, w_out):
    dp_count = lax.axis_size("dp")
    mp_count = lax.axis_size("mp")
    dev_count = dp_count * mp_count
    here_dp = lax.axis_index("dp")
    here_mp = lax.axis_index("mp")
    seq_dev, steps_n, cols_here = history.shape
    seq_total = source.shape[0]
    per_peer = (seq_dev + dp_count - 1) // dp_count
    target = (
        jnp.zeros((seq_total,), jnp.int32).at[source].set(jnp.arange(seq_total, dtype=jnp.int32))
    )
    slot_ids = jnp.arange(seq_dev, dtype=jnp.int32)
    my_seqs = here_dp * seq_dev + slot_ids
    dest_dev = target[my_seqs] // seq_dev
    send_rank = earlier_same(dest_dev)
    outgoing = (
        jnp.zeros((dp_count, per_peer, steps_n, cols_here), jnp.bfloat16)
        .at[dest_dev, send_rank]
        .set(history)
    )
    arrived = lax.all_to_all(outgoing, "dp", split_axis=0, concat_axis=0, tiled=True)
    taken = source[my_seqs]
    anchor = taken // seq_dev
    anchor_block = anchor[:, None] * seq_dev + slot_ids[None, :]
    goes_here = target[anchor_block] // seq_dev == here_dp
    earlier = slot_ids[None, :] < (taken % seq_dev)[:, None]
    recv_rank = jnp.sum((goes_here & earlier).astype(jnp.int32), axis=1)
    counts = lengths[taken]
    local_rows = jnp.take(
        arrived.reshape(dp_count * per_peer, steps_n, cols_here),
        anchor * per_peer + recv_rank,
        axis=0,
    )
    features = lax.all_gather(local_rows, "mp", axis=2, tiled=True)
    rows_all = seq_dev * steps_n
    width = features.shape[2]
    flat_rows = features.reshape(rows_all, width)
    normed = normalize(flat_rows.astype(jnp.float32)).astype(jnp.bfloat16)
    preact = jnp.einsum("rd,cdh->crh", normed, w_in, preferred_element_type=jnp.float32)
    projected = jax.nn.silu(preact).astype(jnp.bfloat16)
    cols_heads = w_in.shape[2]
    heads_here = cols_heads // DH
    grouped = projected.reshape(4, seq_dev, steps_n, heads_here, DH)

    def run_all(inputs):
        return jax.vmap(attend, in_axes=(1, 0))(inputs, counts)

    gated, back = jax.vjp(run_all, grouped)
    gated_flat = gated.reshape(rows_all, cols_heads)
    partial_out = jnp.dot(gated_flat, w_out, preferred_element_type=jnp.float32)
    quarter = rows_all // mp_count
    summed = lax.psum(partial_out, "mp")
    out_rows = lax.dynamic_slice_in_dim(summed, here_mp * quarter, quarter, 0)
    out_rows = out_rows + lax.dynamic_slice_in_dim(flat_rows, here_mp * quarter, quarter, 0).astype(
        jnp.float32
    )
    position = here_mp * quarter + jnp.arange(quarter, dtype=jnp.int32)
    valid_rows = position % steps_n < counts[position // steps_n]
    top_n = owners.shape[1]
    asks = quarter * top_n
    capacity = max(2, (3 * asks + 2 * dev_count - 1) // (2 * dev_count))
    owner_flat = owners.reshape(-1)
    row_flat = item_rows.reshape(-1)
    rank_in = earlier_same(owner_flat)
    address = owner_flat * capacity + rank_in
    slot_table = (
        jnp.full((dev_count * capacity,), asks, jnp.int32)
        .at[address]
        .set(jnp.arange(asks, dtype=jnp.int32))
    )
    is_used = slot_table < asks
    safe_index = jnp.minimum(slot_table, asks - 1)
    wanted = jnp.where(is_used, row_flat[safe_index], 0).reshape(dp_count, mp_count, capacity)
    incoming = lax.all_to_all(
        lax.all_to_all(wanted, "dp", split_axis=0, concat_axis=0, tiled=True),
        "mp",
        split_axis=1,
        concat_axis=1,
        tiled=True,
    )
    incoming_flat = incoming.reshape(-1)
    looked = jnp.take(catalogue, incoming_flat, axis=0).reshape(dp_count, mp_count, capacity, width)
    returned = lax.all_to_all(
        lax.all_to_all(looked, "dp", split_axis=0, concat_axis=0, tiled=True),
        "mp",
        split_axis=1,
        concat_axis=1,
        tiled=True,
    )
    fetched = jnp.take(returned.reshape(dev_count * capacity, width), address, axis=0).reshape(
        quarter, top_n, width
    )
    out_grad, item_grad = loss_block(out_rows, valid_rows, fetched)
    item_flat = item_grad.reshape(asks, width)
    sending = jnp.where(is_used[:, None], jnp.take(item_flat, safe_index, axis=0), 0.0)
    landed = lax.all_to_all(
        lax.all_to_all(
            sending.reshape(dp_count, mp_count, capacity, width).astype(jnp.bfloat16),
            "dp",
            split_axis=0,
            concat_axis=0,
            tiled=True,
        ),
        "mp",
        split_axis=1,
        concat_axis=1,
        tiled=True,
    ).astype(jnp.float32)
    cat_grad = (
        jnp.zeros((catalogue.shape[0], width), jnp.float32)
        .at[incoming_flat]
        .add(landed.reshape(-1, width))
    )
    out_cotangent = lax.all_gather(out_grad.astype(jnp.bfloat16), "mp", axis=0, tiled=True)
    w_out_part = jnp.einsum(
        "rh,rd->hd", gated_flat, out_cotangent, preferred_element_type=jnp.float32
    )
    gated_cotangent = jnp.einsum(
        "rd,hd->rh", out_cotangent, w_out, preferred_element_type=jnp.float32
    ).astype(jnp.bfloat16)
    (grouped_cotangent,) = back(gated_cotangent.reshape(seq_dev, steps_n, heads_here, DH))
    projected_cotangent = grouped_cotangent.reshape(4, rows_all, cols_heads)
    preact_cotangent = (projected_cotangent.astype(jnp.float32) * silu_slope(preact)).astype(
        jnp.bfloat16
    )
    w_in_part = jnp.einsum(
        "rd,crh->cdh", normed, preact_cotangent, preferred_element_type=jnp.float32
    )
    w_in_grad, w_out_grad = (
        lax.psum_scatter(w_in_part, "dp", scatter_dimension=1, tiled=True),
        lax.psum_scatter(w_out_part, "dp", scatter_dimension=1, tiled=True),
    )
    return (w_in_grad, w_out_grad, cat_grad)


def solution(mesh):
    placed = (
        P("dp", None, "mp"),
        P(),
        P(),
        P(("dp", "mp"), None),
        P(("dp", "mp"), None),
        P(("dp", "mp"), None),
        P(None, None, "mp"),
        P("mp", None),
    )
    return jax.shard_map(
        per_device,
        mesh=mesh,
        in_specs=placed,
        out_specs=(P(None, "dp", "mp"), P("mp", "dp"), P(("dp", "mp"), None)),
        check_vma=False,
    )
```

profile of v0, /device:TPU:8, one launch (start us, length us, event | category | flops | bytes accessed | tf_op | source)
XLA Modules:
  0.0 688.2 jit_solution(856039338225278554)
XLA Ops:
  10.0 4.3 scatter_custom_fusion.2
  15.3 5.9 gather_fusion.5
  22.6 11.9 %all-to-all-start.1 = ((s32[64,4,6]{2,1,0:T(4,128)}), s32[64,4,6]{2,1,0:T(4,128)S(1)}, u32[]{:S(2)}, u32[]{:S(2)}) async-start(s32[64,4,6]{2,1,0:T(4,128)} %reshape.655), calls=%async_computation.1 | async-start | bytes 262144 | tf_op jit(solution)/shard_map/all_to_all | solution.py:156
  35.3 4.3 scatter_custom_fusion
  40.4 4.4 all-to-all-done.1
  45.6 4.9 all-to-all-start.2
  51.7 2.7 scatter_fusion
  54.4 6.4 all-to-all-start
  62.7 5.8 gather_fusion.6
  68.6 6.2 gather.53
  74.8 2.6 broadcast_select_fusion
  77.4 7.9 %copy.116 = bf16[64,4,6,1024]{3,1,2,0:T(4,128)(2,1)} copy(bf16[64,4,6,1024]{3,2,1,0:T(8,128)(2,1)S(1)} %broadcast_select_fusion) | data formatting | bytes 6291456 | tf_op jit(solution)/shard_map/jit(_take)/select_n | solution.py:163
  85.2 3.5 all-to-all-done
  88.8 7.2 %all-to-all-start.3 = ((bf16[64,4,6,1024]{3,1,2,0:T(4,128)(2,1)}), bf16[64,4,6,1024]{3,1,2,0:T(4,128)(2,1)}, u32[]{:S(2)}, u32[]{:S(2)}) async-start(bf16[64,4,6,1024]{3,1,2,0:T(4,128)(2,1)} %copy.116), calls=%async_computation.3 | async-start | bytes 6291456 | tf_op jit(solution)/shard_map/all_to_all | solution.py:165
  101.8 27.1 %all-gather.3.cloned.1.call-done = bf16[16,32,1024]{2,1,0:T(8,128)(2,1)} async-done(((bf16[16,32,256]{2,1,0:T(8,128)(2,1)}), bf16[16,32,1024]{2,1,0:T(8,128)(2,1)}) %all-gather.3.cloned.1.call-update) | async-done | bytes 1048592 | tf_op jit(solution)/shard_map/all_gather | solution.py:115
  132.2 2.8 fusion.16
  138.9 1.8 fusion.54
  140.8 27.9 %all-to-all-done.3 = bf16[64,4,6,1024]{3,1,2,0:T(4,128)(2,1)} async-done(((bf16[64,4,6,1024]{3,1,2,0:T(4,128)(2,1)}), bf16[64,4,6,1024]{3,1,2,0:T(4,128)(2,1)}, u32[]{:S(2)}, u32[]{:S(2)}) %all-to-all-start.3) | async-done | bytes 3145760 | tf_op jit(solution)/shard_map/all_to_all | solution.py:165
  168.6 5.3 copy.117
  173.9 5.4 all-to-all-start.4
  183.5 1.9 fusion.89
  185.5 10.0 %compare_convert_fusion = f32[128]{0:T(128)S(1)} fusion(s32[]{:T(128)} %bitcast.39, s32[]{:T(128)} %bitcast.40, s32[]{:T(128)} %bitcast.41, s32[]{:T(128)} %bitcast.42, s32[]{:T(128)} %bitcast.43, s32[]{:T(128)} %bitcast.45, s32[]{:T(128)} %bitcast.44, s32[]{:T(128)} %bitcast.22, s32[]{:T(128)} %bitcast.24, s32[]{:T(128)} %bitcast.26, s32[]{:T(128)} %bitcast.28, ...), kind=kLoop, calls=%fused_computation.196 | loop fusion | flops 8064 | bytes 580 | tf_op jit(solution)/shard_map/convert_element_type | solution.py:50
  196.8 34.2 %all-reduce.8.cloned.1.call-done = f32[512,1024]{1,0:T(8,128)} async-done(((f32[512,1024]{1,0:T(8,128)}), f32[512,1024]{1,0:T(8,128)}) %all-reduce.8.cloned.1.call-update) | async-done | bytes 2097168 | tf_op jit(solution)/shard_map/psum | solution.py:133
  232.3 2.0 fusion.50
  234.4 3.7 copy.118
  238.1 4.9 reshape.657
  243.0 5.3 gather_fusion.7
  248.3 2.5 fusion.2
  250.9 2.8 fusion.10
  259.0 5.8 gather_fusion.8
  264.8 6.2 gather.58
  271.1 4.7 fusion.1
  275.8 4.2 copy.133
  279.9 5.8 all-to-all-start.5
  286.9 28.9 %all-gather.5.cloned.1.call-done = bf16[512,1024]{1,0:T(8,128)(2,1)} async-done(((bf16[128,1024]{1,0:T(8,128)(2,1)}), bf16[512,1024]{1,0:T(8,128)(2,1)}) %all-gather.5.cloned.1.call-update) | async-done | bytes 1048592 | tf_op jit(solution)/shard_map/all_gather | solution.py:195
  321.2 1.9 copy.127
  323.2 2.8 reshape.662
  326.0 6.1 convolution_bitcast_fusion
  332.2 5.2 copy.129
  337.4 21.5 %all-to-all-done.5 = bf16[64,4,6,1024]{3,1,2,0:T(4,128)(2,1)} async-done(((bf16[64,4,6,1024]{3,1,2,0:T(4,128)(2,1)}), bf16[64,4,6,1024]{3,1,2,0:T(4,128)(2,1)}, u32[]{:S(2)}, u32[]{:S(2)}) %all-to-all-start.5) | async-done | bytes 3145760 | tf_op jit(solution)/shard_map/all_to_all | solution.py:178
  358.9 5.4 copy.134
  364.3 6.6 all-to-all-start.6
  370.9 2.8 fusion.52
  375.0 163.0 %all-reduce.10.cloned.1.call-done = f32[4,1024,256]{2,0,1:T(4,128)} async-done(((f32[4,1024,256]{2,0,1:T(4,128)}), f32[4,1024,256]{2,0,1:T(4,128)}) %all-reduce.10.cloned.1.call-update) | async-done | bytes 4194320
  539.4 5.1 copy.135
  544.6 8.4 %reshape.790 = f32[1536,1024]{1,0:T(8,128)} reshape(f32[64,4,6,1024]{3,2,1,0:T(8,128)} %copy.135) | data formatting | bytes 12582912 | tf_op jit(solution)/shard_map/reshape | solution.py:193
  553.0 16.1 %scatter_custom_fusion.3 = f32[512,1024]{1,0:T(8,128)} fusion(s32[1536]{0:T(1024)} %copy-done.39, f32[1536,1024]{1,0:T(8,128)} %reshape.790, f32[]{:T(128)} %constant.182.clone.1), kind=kCustom, calls=%fused_computation.68 | custom fusion | flops 1572864 | bytes 2097664 | tf_op jit(solution)/shard_map/scatter-add | solution.py:193
  569.1 112.4 %reduce-scatter.2.cloned.1.call-done = f32[256,16]{0,1:T(8,128)} async-done(((f32[256,1024]{0,1:T(8,128)}), f32[256,16]{0,1:T(8,128)}) %reduce-scatter.2.cloned.1.call-update) | async-done | bytes 16400 | tf_op jit(solution)/shard_map/reduce_scatter | solution.py:212
  (219 shorter events, 44.1 us)
Async XLA Ops:
  7.2 125.0 %copy-start = (bf16[4,1024,256]{2,1,0:T(8,128)(2,1)S(1)}, bf16[4,1024,256]{2,1,0:T(8,128)(2,1)}, u32[]{:S(2)}) copy-start(bf16[4,1024,256]{2,1,0:T(8,128)(2,1)} %param.14) | copy-start | bytes 6291460
  9.3 5.1 copy-start.38
  14.4 6.8 copy-start.29
  14.4 6.8 copy-start.30
  15.3 19.3 %copy-start.3 = (s32[1024]{0:T(1024)S(1)}, s32[1024]{0:T(1024)}, u32[]{:S(2)}) copy-start(s32[1024]{0:T(1024)} %param.10) | copy-start | bytes 12292
  22.6 22.2 %all-to-all-start.1 = ((s32[64,4,6]{2,1,0:T(4,128)}), s32[64,4,6]{2,1,0:T(4,128)S(1)}, u32[]{:S(2)}, u32[]{:S(2)}) async-start(s32[64,4,6]{2,1,0:T(4,128)} %reshape.655), calls=%async_computation.1 | async-start | bytes 262144 | tf_op jit(solution)/shard_map/all_to_all | solution.py:156
  45.6 8.8 %all-to-all-start.2 = ((s32[4,1,384]{2,1,0:T(1,128)}), s32[4,1,384]{2,1,0:T(1,128)S(1)}, u32[]{:S(2)}, u32[]{:S(2)}) async-start(s32[4,1,384]{2,1,0:T(1,128)} %reshape.856), calls=%async_computation.2 | async-start | bytes 12288 | tf_op jit(solution)/shard_map/all_to_all | solution.py:155
  50.6 12.2 %copy-start.2 = (bf16[512,1024]{1,0:T(8,128)(2,1)S(1)}, bf16[512,1024]{1,0:T(8,128)(2,1)}, u32[]{:S(2)}) copy-start(bf16[512,1024]{1,0:T(8,128)(2,1)} %param.13) | copy-start | bytes 3145732
  54.4 34.4 %all-to-all-start = ((bf16[64,1,32,256]{3,2,1,0:T(8,128)(2,1)}), bf16[64,1,32,256]{3,2,1,0:T(8,128)(2,1)}, u32[]{:S(2)}, u32[]{:S(2)}) async-start(bf16[64,1,32,256]{3,2,1,0:T(8,128)(2,1)} %bitcast.239), calls=%async_computation | async-start | bytes 2097152 | tf_op jit(solution)/shard_map/all_to_all | solution.py:102
  62.7 5.9 copy-start.39
  88.8 79.9 %all-to-all-start.3 = ((bf16[64,4,6,1024]{3,1,2,0:T(4,128)(2,1)}), bf16[64,4,6,1024]{3,1,2,0:T(4,128)(2,1)}, u32[]{:S(2)}, u32[]{:S(2)}) async-start(bf16[64,4,6,1024]{3,1,2,0:T(4,128)(2,1)} %copy.116), calls=%async_computation.3 | async-start | bytes 6291456 | tf_op jit(solution)/shard_map/all_to_all | solution.py:165
  95.9 32.9 %all-gather.3.cloned.1.call-start = ((), (), s32[]{:S(2)}) async-start(), calls=%async_computation.8 | async-start | bytes 1310720 | tf_op jit(solution)/shard_map/all_gather | solution.py:115
  96.0 4.6 copy-start.4
  100.3 130.8 %all-reduce.8.cloned.1.call-start = ((), (), s32[]{:S(2)}) async-start(), calls=%async_computation.9 | async-start | bytes 4194304 | tf_op jit(solution)/shard_map/psum | solution.py:133
  101.2 34.4 %copy-start.47 = (f32[16]{0:T(128)}, f32[16]{0:T(128)S(1)}, u32[]{:S(2)}) copy-start(f32[16]{0:T(128)S(1)} %convert_element_type.130) | copy-start | bytes 196
  101.8 33.9 %copy-start.34 = (pred[16,32,32]{2,1,0:T(8,128)(4,1)}, pred[16,32,32]{2,1,0:T(8,128)(4,1)S(1)}, u32[]{:S(2)}) copy-start(pred[16,32,32]{2,1,0:T(8,128)(4,1)S(1)} %broadcast_and_fusion) | copy-start | bytes 49156
  128.8 3.4 copy-start.12
  130.4 4.6 copy-start.42
  132.2 2.8 copy-start.44
  135.2 1.6 copy-start.20
  135.6 2.6 copy-start.10
  136.8 4.0 copy-start.22
  136.8 2.1 copy-start.14
  138.3 2.5 copy-start.25
  173.9 60.4 %all-to-all-start.4 = ((bf16[64,4,6,1024]{3,0,2,1:T(8,128)(2,1)}), bf16[64,4,6,1024]{3,0,2,1:T(8,128)(2,1)S(1)}, u32[]{:S(2)}, u32[]{:S(2)}) async-start(bf16[64,4,6,1024]{3,0,2,1:T(8,128)(2,1)} %copy.117), calls=%async_computation.4 | async-start | bytes 6291456 | tf_op jit(solution)/shard_map/all_to_all | solution.py:164
  248.3 2.6 copy-start.5
  248.3 2.6 copy-start.33
  250.9 2.8 copy-start.36
  250.9 3.1 copy-start.9
  254.0 1.7 copy-start.37
  255.7 1.6 copy-start.6
  257.3 1.7 copy-start.31
  279.9 79.0 %all-to-all-start.5 = ((bf16[64,4,6,1024]{3,1,2,0:T(4,128)(2,1)}), bf16[64,4,6,1024]{3,1,2,0:T(4,128)(2,1)}, u32[]{:S(2)}, u32[]{:S(2)}) async-start(bf16[64,4,6,1024]{3,1,2,0:T(4,128)(2,1)} %copy.133), calls=%async_computation.6 | async-start | bytes 6291456 | tf_op jit(solution)/shard_map/all_to_all | solution.py:178
  285.7 30.1 %copy-start.15 = (bf16[256,1024]{1,0:T(8,128)(2,1)S(1)}, bf16[256,1024]{1,0:T(8,128)(2,1)}, u32[]{:S(2)}) copy-start(bf16[256,1024]{1,0:T(8,128)(2,1)} %param.15) | copy-start | bytes 1572868
  285.7 30.1 %all-gather.5.cloned.1.call-start = ((), (), s32[]{:S(2)}) async-start(), calls=%async_computation.10 | async-start | bytes 1310720 | tf_op jit(solution)/shard_map/all_gather | solution.py:195
  286.0 31.9 %copy-start.8 = (f32[16,32,2,128]{3,1,2,0:T(8,128)S(1)}, f32[16,32,2,128]{3,1,2,0:T(8,128)}, u32[]{:S(2)}) copy-start(f32[16,32,2,128]{3,1,2,0:T(8,128)} %copy-done.7) | copy-start | bytes 1572868
  286.0 31.9 %copy-start.11 = (f32[16,32,2,128]{3,2,1,0:T(2,128)S(1)}, f32[16,32,2,128]{3,2,1,0:T(2,128)}, u32[]{:S(2)}) copy-start(f32[16,32,2,128]{3,2,1,0:T(2,128)} %copy-done.10) | copy-start | bytes 1572868
  286.0 31.9 %copy-start.32 = (f32[16,32,2]{1,2,0:T(2,128)S(1)}, f32[16,32,2]{1,2,0:T(2,128)}, u32[]{:S(2)}) copy-start(f32[16,32,2]{1,2,0:T(2,128)} %get-tuple-element.29) | copy-start | bytes 12292
  286.9 31.5 %copy-start.28 = (f32[16,32,2]{1,2,0:T(2,128)S(1)}, f32[16,32,2]{1,2,0:T(2,128)}, u32[]{:S(2)}) copy-start(f32[16,32,2]{1,2,0:T(2,128)} %copy-done.27) | copy-start | bytes 12292
  286.9 31.6 %copy-start.26 = (f32[16,32,2]{1,2,0:T(2,128)S(1)}, f32[16,32,2]{1,2,0:T(2,128)}, u32[]{:S(2)}) copy-start(f32[16,32,2]{1,2,0:T(2,128)} %copy-done.25) | copy-start | bytes 12292
  286.9 251.1 %all-reduce.10.cloned.1.call-start = ((), (), s32[]{:S(2)}) async-start(), calls=%async_computation.12 | async-start | bytes 8388608
  323.2 2.9 copy-start.13
  323.2 2.9 copy-start.43
  323.2 2.9 copy-start.45
  364.3 175.2 %all-to-all-start.6 = ((bf16[64,4,6,1024]{3,0,2,1:T(8,128)(2,1)}), bf16[64,4,6,1024]{3,0,2,1:T(8,128)(2,1)S(1)}, u32[]{:S(2)}, u32[]{:S(2)}) async-start(bf16[64,4,6,1024]{3,0,2,1:T(8,128)(2,1)} %copy.134), calls=%async_computation.7 | async-start | bytes 6291456 | tf_op jit(solution)/shard_map/all_to_all | solution.py:177
  370.9 2.8 copy-start.46
  370.9 310.6 %reduce-scatter.2.cloned.1.call-start = ((), (), s32[]{:S(2)}) async-start(), calls=%async_computation.11 | async-start | bytes 1064960 | tf_op jit(solution)/shard_map/reduce_scatter | solution.py:212
  544.6 136.9 %copy-start.1 = (bf16[4,1024,256]{2,1,0:T(8,128)(2,1)S(1)}, bf16[4,1024,256]{2,1,0:T(8,128)(2,1)}, u32[]{:S(2)}) copy-start(bf16[4,1024,256]{2,1,0:T(8,128)(2,1)} %param.14) | copy-start | bytes 6291460
  (14 other events, 15.4 us)
Sparse Core Ops, SparseCore 0:
  100.4 28.3 all-gather.2
  140.9 90.1 all-reduce.7
  288.3 27.4 all-gather.4
  337.5 200.3 all-reduce.9
  542.4 139.0 reduce-scatter.1
where the time goes:
time: 695 us; the launch traced here: 688 us
  waiting for transfers between devices  423 us (61%)
  local copies, waits for them, and re-layouts  123 us (18%)
  other arithmetic  55.8 us (8%)
  starting transfers between devices  48.5 us (7%)
  matrix products  21.9 us (3%)
  between operations  15.7 us (2%)
    unnamed x6, waiting for transfers between devices  163 us
    reduce_scatter x1, waiting for transfers between devices, per_device(): lax.psum_scatter(w_out_part, 'dp', scatter_dimension=1, tiled=True)  112 us
    psum x1, waiting for transfers between devices, per_device(): summed = lax.psum(partial_out, 'mp')  34.2 us
    all_gather x1, waiting for transfers between devices, per_device(): lax.all_gather(out_grad.astype(jnp.bfloat16), 'mp', axis=0, tiled=True)  28.9 us
    all_to_all x1, waiting for transfers between devices, per_device(): lax.all_to_all(looked, 'dp', split_axis=0, concat_axis=0, tiled=True)  27.9 us
    all_gather x1, waiting for transfers between devices, per_device(): features = lax.all_gather(local_rows, 'mp', axis=2, tiled=True)  27.1 us
    all_to_all x1, waiting for transfers between devices, per_device(): lax.all_to_all(sending.reshape(dp_count, mp_count, capacity, width).astyp...  21.5 us
    scatter-add x1, other arithmetic, per_device(): cat_grad = jnp.zeros((catalogue.shape[0], width), jnp.float32).at[incomin...  16.1 us
  transfers between devices with their start and end apart: 12, of which 9 were waited for; matrix products, arithmetic and copies ran while one was open for 20% of the time, Pallas kernels for 0%

commit v1 on v0

--- a/solution.py
+++ b/solution.py
@@ -130,7 +130,9 @@
     gated_flat = gated.reshape(rows_all, cols_heads)
     partial_out = jnp.dot(gated_flat, w_out, preferred_element_type=jnp.float32)
     quarter = rows_all // mp_count
-    summed = lax.psum(partial_out, "mp")
+    summed = partial_out
+    for hop in (1, 2):
+        summed = summed + lax.ppermute(summed, "mp", [(dev, dev ^ hop) for dev in range(4)])
     out_rows = lax.dynamic_slice_in_dim(summed, here_mp * quarter, quarter, 0)
     out_rows = out_rows + lax.dynamic_slice_in_dim(flat_rows, here_mp * quarter, quarter, 0).astype(
         jnp.float32

time: 695 us -> 726 us (1.045)
  waiting for transfers between devices: 423 us -> 447 us
    ppermute x0 -> x2, waiting for transfers between devices: none -> 54 us  [per_device(): lax.ppermute(summed, 'mp', [(dev, dev ^ hop) for dev in range(4)])]
    psum x1 -> x0, waiting for transfers between devices: 34.2 us -> none  [per_device(): summed = lax.psum(partial_out, 'mp')]
    all_to_all x1, waiting for transfers between devices: 0.01 us -> 28.3 us  [per_device(): lax.all_to_all(lax.all_to_all(looked, 'dp', split_axis=0, concat_axis=0,...]
    all_gather x1, waiting for transfers between devices: 27.1 us -> 0.02 us  [per_device(): features = lax.all_gather(local_rows, 'mp', axis=2, tiled=True)]
    all_to_all x1, waiting for transfers between devices: 27.9 us -> 11.1 us  [per_device(): lax.all_to_all(looked, 'dp', split_axis=0, concat_axis=0, tiled=True)]
    all_to_all x1, waiting for transfers between devices: 3.51 us -> 14.7 us  [per_device(): lax.all_to_all(outgoing, 'dp', split_axis=0, concat_axis=0, tiled=True)]
    unnamed x6 -> x5, waiting for transfers between devices: 163 us -> 162 us
  transfers between devices with their start and end apart: 12 -> 13, of which waited for: 9 -> 11; matrix products, arithmetic and copies ran while one was open for 20% -> 20% of each run, Pallas kernels for 0% -> 0%
where the time goes in v1:
time: 726 us; the launch traced here: 719 us
  waiting for transfers between devices  447 us (62%)
  local copies, waits for them, and re-layouts  120 us (17%)
  other arithmetic  60.3 us (8%)
  starting transfers between devices  54.4 us (7%)
  matrix products  21.4 us (3%)
  between operations  15.7 us (2%)
    unnamed x5, waiting for transfers between devices  162 us
    reduce_scatter x1, waiting for transfers between devices, per_device(): lax.psum_scatter(w_out_part, 'dp', scatter_dimension=1, tiled=True)  112 us
    ppermute x2, waiting for transfers between devices, per_device(): lax.ppermute(summed, 'mp', [(dev, dev ^ hop) for dev in range(4)])  54 us
    all_to_all x1, waiting for transfers between devices, per_device(): lax.all_to_all(lax.all_to_all(looked, 'dp', split_axis=0, concat_axis=0,...  28.3 us
    all_gather x1, waiting for transfers between devices, per_device(): lax.all_gather(out_grad.astype(jnp.bfloat16), 'mp', axis=0, tiled=True)  26.8 us
    all_to_all x1, waiting for transfers between devices, per_device(): lax.all_to_all(sending.reshape(dp_count, mp_count, capacity, width).astyp...  24.6 us
    scatter-add x1, other arithmetic, per_device(): cat_grad = jnp.zeros((catalogue.shape[0], width), jnp.float32).at[incomin...  16.1 us
    all_to_all x1, waiting for transfers between devices, per_device(): lax.all_to_all(outgoing, 'dp', split_axis=0, concat_axis=0, tiled=True)  14.7 us
  transfers between devices with their start and end apart: 13, of which 11 were waited for; matrix products, arithmetic and copies ran while one was open for 20% of the time, Pallas kernels for 0%

profile of v1, /device:TPU:8, one launch (start us, length us, event | category | flops | bytes accessed | tf_op | source)
XLA Modules:
  0.0 719.2 jit_solution(6678038253761618875)
XLA Ops:
  9.4 4.3 scatter_custom_fusion
  15.7 2.5 scatter_fusion
  18.2 12.2 %all-to-all-start = ((bf16[64,1,32,256]{3,2,1,0:T(8,128)(2,1)}), bf16[64,1,32,256]{3,2,1,0:T(8,128)(2,1)}, u32[]{:S(2)}, u32[]{:S(2)}) async-start(bf16[64,1,32,256]{3,2,1,0:T(8,128)(2,1)} %bitcast.7), calls=%async_computation | async-start | bytes 2097152 | tf_op jit(solution)/shard_map/all_to_all | solution.py:102
  33.2 4.3 scatter_custom_fusion.2
  37.5 5.9 gather_fusion.5
  43.6 14.7 %all-to-all-done = bf16[64,1,32,256]{3,2,1,0:T(8,128)(2,1)} async-done(((bf16[64,1,32,256]{3,2,1,0:T(8,128)(2,1)}), bf16[64,1,32,256]{3,2,1,0:T(8,128)(2,1)}, u32[]{:S(2)}, u32[]{:S(2)}) %all-to-all-start) | async-done | bytes 1048608 | tf_op jit(solution)/shard_map/all_to_all | solution.py:102
  62.4 6.6 all-to-all-start.1
  69.0 10.3 %all-to-all-done.1 = s32[64,4,6]{2,1,0:T(4,128)S(1)} async-done(((s32[64,4,6]{2,1,0:T(4,128)}), s32[64,4,6]{2,1,0:T(4,128)S(1)}, u32[]{:S(2)}, u32[]{:S(2)}) %all-to-all-start.1) | async-done | bytes 6176 | tf_op jit(solution)/shard_map/all_to_all | solution.py:158
  80.0 5.1 all-to-all-start.2
  85.8 3.2 all-to-all-done.2
  90.8 5.8 gather_fusion.6
  96.6 6.2 gather.53
  102.8 2.6 broadcast_select_fusion
  105.4 7.9 %copy.116 = bf16[64,4,6,1024]{3,1,2,0:T(4,128)(2,1)} copy(bf16[64,4,6,1024]{3,2,1,0:T(8,128)(2,1)S(1)} %broadcast_select_fusion) | data formatting | bytes 6291456 | tf_op jit(solution)/shard_map/jit(_take)/select_n | solution.py:165
  113.2 5.8 all-to-all-start.3
  122.6 2.8 fusion.16
  131.2 46.1 %collective-permute-done = f32[512,1024]{1,0:T(8,128)S(1)} collective-permute-done((f32[512,1024]{1,0:T(8,128)S(1)}, f32[512,1024]{1,0:T(8,128)S(1)}, u32[]{:S(2)}, u32[]{:S(2)}) %collective-permute-start) | collective-permute-done | bytes 2097184 | tf_op jit(solution)/shard_map/ppermute | solution.py:135
  180.6 11.1 %all-to-all-done.3 = bf16[64,4,6,1024]{3,1,2,0:T(4,128)(2,1)} async-done(((bf16[64,4,6,1024]{3,1,2,0:T(4,128)(2,1)}), bf16[64,4,6,1024]{3,1,2,0:T(4,128)(2,1)}, u32[]{:S(2)}, u32[]{:S(2)}) %all-to-all-start.3) | async-done | bytes 3145760 | tf_op jit(solution)/shard_map/all_to_all | solution.py:167
  191.7 5.2 copy.117
  197.0 5.5 all-to-all-start.4
  209.2 10.5 %compare_convert_fusion = f32[128]{0:T(128)} fusion(s32[]{:T(128)} %bitcast.39, s32[]{:T(128)} %bitcast.40, s32[]{:T(128)} %bitcast.41, s32[]{:T(128)} %bitcast.42, s32[]{:T(128)} %bitcast.43, s32[]{:T(128)} %bitcast.45, s32[]{:T(128)} %bitcast.44, s32[]{:T(128)} %bitcast.22, s32[]{:T(128)} %bitcast.24, s32[]{:T(128)} %bitcast.26, s32[]{:T(128)} %bitcast.28, ...), kind=kLoop, calls=%fused_computation.197 | loop fusion | flops 8064 | bytes 580 | tf_op jit(solution)/shard_map/convert_element_type | solution.py:50
  221.7 7.9 %collective-permute-done.1 = f32[512,1024]{1,0:T(8,128)} collective-permute-done((f32[512,1024]{1,0:T(8,128)}, f32[512,1024]{1,0:T(8,128)}, u32[]{:S(2)}, u32[]{:S(2)}) %collective-permute-start.1) | collective-permute-done | bytes 2097184 | tf_op jit(solution)/shard_map/ppermute | solution.py:135
  231.0 2.2 broadcast_divide_fusion
  233.2 28.3 %all-to-all-done.4 = bf16[64,4,6,1024]{3,0,2,1:T(8,128)(2,1)S(1)} async-done(((bf16[64,4,6,1024]{3,0,2,1:T(8,128)(2,1)}), bf16[64,4,6,1024]{3,0,2,1:T(8,128)(2,1)S(1)}, u32[]{:S(2)}, u32[]{:S(2)}) %all-to-all-start.4) | async-done | bytes 3145760 | tf_op jit(solution)/shard_map/all_to_all | solution.py:166
  261.5 3.7 copy.118
  265.2 4.9 reshape.657
  270.1 5.3 gather_fusion.7
  275.4 2.5 fusion.2
  278.1 2.8 fusion.10
  286.6 5.8 gather_fusion.8
  292.4 6.2 gather.58
  298.6 4.4 fusion.1
  303.0 4.2 copy.133
  307.2 10.9 %all-to-all-start.5 = ((bf16[64,4,6,1024]{3,1,2,0:T(4,128)(2,1)}), bf16[64,4,6,1024]{3,1,2,0:T(4,128)(2,1)}, u32[]{:S(2)}, u32[]{:S(2)}) async-start(bf16[64,4,6,1024]{3,1,2,0:T(4,128)(2,1)} %copy.133), calls=%async_computation.6 | async-start | bytes 6291456 | tf_op jit(solution)/shard_map/all_to_all | solution.py:180
  319.4 26.8 %all-gather.5.cloned.1.call-done = bf16[512,1024]{1,0:T(8,128)(2,1)} async-done(((bf16[128,1024]{1,0:T(8,128)(2,1)}), bf16[512,1024]{1,0:T(8,128)(2,1)}) %all-gather.5.cloned.1.call-update) | async-done | bytes 1048592 | tf_op jit(solution)/shard_map/all_gather | solution.py:197
  351.6 1.9 copy.127
  353.5 2.9 reshape.662
  356.4 6.1 convolution_bitcast_fusion
  362.6 5.2 copy.129
  367.8 24.6 %all-to-all-done.5 = bf16[64,4,6,1024]{3,1,2,0:T(4,128)(2,1)} async-done(((bf16[64,4,6,1024]{3,1,2,0:T(4,128)(2,1)}), bf16[64,4,6,1024]{3,1,2,0:T(4,128)(2,1)}, u32[]{:S(2)}, u32[]{:S(2)}) %all-to-all-start.5) | async-done | bytes 3145760 | tf_op jit(solution)/shard_map/all_to_all | solution.py:180
  392.4 5.3 copy.134
  397.8 5.2 all-to-all-start.6
  403.0 2.8 fusion.52
  407.1 161.9 %all-reduce.7.cloned.1.call-done = f32[4,1024,256]{2,0,1:T(4,128)} async-done(((f32[4,1024,256]{2,0,1:T(4,128)}), f32[4,1024,256]{2,0,1:T(4,128)}) %all-reduce.7.cloned.1.call-update) | async-done | bytes 4194320
  570.5 5.2 copy.135
  575.6 8.4 %reshape.790 = f32[1536,1024]{1,0:T(8,128)} reshape(f32[64,4,6,1024]{3,2,1,0:T(8,128)} %copy.135) | data formatting | bytes 12582912 | tf_op jit(solution)/shard_map/reshape | solution.py:195
  584.1 16.1 %scatter_custom_fusion.3 = f32[512,1024]{1,0:T(8,128)} fusion(s32[1536]{0:T(1024)S(1)} %fusion.73, f32[1536,1024]{1,0:T(8,128)} %reshape.790, f32[]{:T(128)} %constant.182.clone.1), kind=kCustom, calls=%fused_computation.68 | custom fusion | flops 1572864 | bytes 2097664 | tf_op jit(solution)/shard_map/scatter-add | solution.py:195
  600.1 112.3 %reduce-scatter.2.cloned.1.call-done = f32[256,16]{0,1:T(8,128)} async-done(((f32[256,1024]{0,1:T(8,128)}), f32[256,16]{0,1:T(8,128)}) %reduce-scatter.2.cloned.1.call-update) | async-done | bytes 16400 | tf_op jit(solution)/shard_map/reduce_scatter | solution.py:214
  (223 shorter events, 51.2 us)
Async XLA Ops:
  7.2 115.4 %copy-start = (bf16[4,1024,256]{2,1,0:T(8,128)(2,1)S(1)}, bf16[4,1024,256]{2,1,0:T(8,128)(2,1)}, u32[]{:S(2)}) copy-start(bf16[4,1024,256]{2,1,0:T(8,128)(2,1)} %param.14) | copy-start | bytes 6291460
  7.2 8.5 %copy-start.23 = (bf16[16,32,256]{2,1,0:T(8,128)(2,1)S(1)}, bf16[16,32,256]{2,1,0:T(8,128)(2,1)}, u32[]{:S(2)}) copy-start(bf16[16,32,256]{2,1,0:T(8,128)(2,1)} %param.8) | copy-start | bytes 786436
  18.2 40.2 %all-to-all-start = ((bf16[64,1,32,256]{3,2,1,0:T(8,128)(2,1)}), bf16[64,1,32,256]{3,2,1,0:T(8,128)(2,1)}, u32[]{:S(2)}, u32[]{:S(2)}) async-start(bf16[64,1,32,256]{3,2,1,0:T(8,128)(2,1)} %bitcast.7), calls=%async_computation | async-start | bytes 2097152 | tf_op jit(solution)/shard_map/all_to_all | solution.py:102
  30.4 88.8 %all-gather.3.cloned.1.call-start = ((), (), s32[]{:S(2)}) async-start(), calls=%async_computation.8 | async-start | bytes 1310720 | tf_op jit(solution)/shard_map/all_gather | solution.py:115
  33.1 4.4 copy-start.33
  43.4 41.7 %copy-start.3 = (s32[1024]{0:T(1024)S(1)}, s32[1024]{0:T(1024)}, u32[]{:S(2)}) copy-start(s32[1024]{0:T(1024)} %param.9) | copy-start | bytes 12292
  43.4 47.4 %copy-start.2 = (bf16[512,1024]{1,0:T(8,128)(2,1)S(1)}, bf16[512,1024]{1,0:T(8,128)(2,1)}, u32[]{:S(2)}) copy-start(bf16[512,1024]{1,0:T(8,128)(2,1)} %param.13) | copy-start | bytes 3145732
  62.4 16.9 %all-to-all-start.1 = ((s32[64,4,6]{2,1,0:T(4,128)}), s32[64,4,6]{2,1,0:T(4,128)S(1)}, u32[]{:S(2)}, u32[]{:S(2)}) async-start(s32[64,4,6]{2,1,0:T(4,128)} %reshape.655), calls=%async_computation.1 | async-start | bytes 262144 | tf_op jit(solution)/shard_map/all_to_all | solution.py:158
  80.0 8.9 %all-to-all-start.2 = ((s32[4,1,384]{2,1,0:T(1,128)}), s32[4,1,384]{2,1,0:T(1,128)S(1)}, u32[]{:S(2)}, u32[]{:S(2)}) async-start(s32[4,1,384]{2,1,0:T(1,128)} %reshape.856), calls=%async_computation.2 | async-start | bytes 12288 | tf_op jit(solution)/shard_map/all_to_all | solution.py:157
  85.8 40.2 %copy-start.48 = (f32[16]{0:T(128)}, f32[16]{0:T(128)S(1)}, u32[]{:S(2)}) copy-start(f32[16]{0:T(128)S(1)} %convert_element_type.130) | copy-start | bytes 196
  113.2 78.5 %all-to-all-start.3 = ((bf16[64,4,6,1024]{3,1,2,0:T(4,128)(2,1)}), bf16[64,4,6,1024]{3,1,2,0:T(4,128)(2,1)}, u32[]{:S(2)}, u32[]{:S(2)}) async-start(bf16[64,4,6,1024]{3,1,2,0:T(4,128)(2,1)} %copy.116), calls=%async_computation.3 | async-start | bytes 6291456 | tf_op jit(solution)/shard_map/all_to_all | solution.py:167
  119.1 6.8 copy-start.26
  119.2 3.4 copy-start.11
  120.8 4.6 copy-start.42
  122.5 2.8 copy-start.44
  126.0 2.6 copy-start.9
  127.1 2.5 copy-start.21
  127.1 2.1 copy-start.13
  127.5 2.2 copy-start.7
  129.7 47.7 %collective-permute-start = (f32[512,1024]{1,0:T(8,128)S(1)}, f32[512,1024]{1,0:T(8,128)S(1)}, u32[]{:S(2)}, u32[]{:S(2)}) collective-permute-start(f32[512,1024]{1,0:T(8,128)S(1)} %fusion.54), channel_id=1, source_target_pairs={{0,1},{1,0},{2,3},{3,2},{4,5},{5,4},{6,7},{7,6},{8,9},{9,8},{10,11... | collective-permute-start | bytes 6291464 | tf_op jit(solution)/shard_map/ppermute | solution.py:135
  179.2 50.4 %collective-permute-start.1 = (f32[512,1024]{1,0:T(8,128)}, f32[512,1024]{1,0:T(8,128)}, u32[]{:S(2)}, u32[]{:S(2)}) collective-permute-start(f32[512,1024]{1,0:T(8,128)} %add.411), channel_id=1, source_target_pairs={{0,2},{1,3},{2,0},{3,1},{4,6},{5,7},{6,4},{7,5},{8,10},{9,11},{10,... | collective-permute-start | bytes 6291464 | tf_op jit(solution)/shard_map/ppermute | solution.py:135
  197.0 64.5 %all-to-all-start.4 = ((bf16[64,4,6,1024]{3,0,2,1:T(8,128)(2,1)}), bf16[64,4,6,1024]{3,0,2,1:T(8,128)(2,1)S(1)}, u32[]{:S(2)}, u32[]{:S(2)}) async-start(bf16[64,4,6,1024]{3,0,2,1:T(8,128)(2,1)} %copy.117), calls=%async_computation.4 | async-start | bytes 6291456 | tf_op jit(solution)/shard_map/all_to_all | solution.py:166
  205.5 69.9 %copy-start.34 = (pred[1024]{0:T(1024)(128)(4,1)}, pred[1024]{0:T(1024)(128)(4,1)S(1)}, u32[]{:S(2)}) copy-start(pred[1024]{0:T(1024)(128)(4,1)S(1)} %broadcast_in_dim.164) | copy-start | bytes 3076
  231.0 34.2 %copy-start.39 = (f32[128]{0:T(128)}, f32[128]{0:T(128)S(1)}, u32[]{:S(2)}) copy-start(f32[128]{0:T(128)S(1)} %add_sqrt_fusion.2) | copy-start | bytes 1540
  275.4 2.6 copy-start.4
  275.4 2.6 copy-start.25
  278.0 2.8 copy-start.28
  278.1 2.9 copy-start.41
  278.1 2.9 copy-start.46
  278.1 3.1 copy-start.6
  278.1 3.1 copy-start.35
  292.4 6.2 copy-start.30
  292.4 6.2 copy-start.31
  307.2 11.2 %copy-start.40 = (f32[128]{0:T(128)S(1)}, f32[128]{0:T(128)}, u32[]{:S(2)}) copy-start(f32[128]{0:T(128)} %copy-done.39) | copy-start | bytes 1540
  307.2 85.2 %all-to-all-start.5 = ((bf16[64,4,6,1024]{3,1,2,0:T(4,128)(2,1)}), bf16[64,4,6,1024]{3,1,2,0:T(4,128)(2,1)}, u32[]{:S(2)}, u32[]{:S(2)}) async-start(bf16[64,4,6,1024]{3,1,2,0:T(4,128)(2,1)} %copy.133), calls=%async_computation.6 | async-start | bytes 6291456 | tf_op jit(solution)/shard_map/all_to_all | solution.py:180
  318.1 28.0 %copy-start.14 = (bf16[256,1024]{1,0:T(8,128)(2,1)S(1)}, bf16[256,1024]{1,0:T(8,128)(2,1)}, u32[]{:S(2)}) copy-start(bf16[256,1024]{1,0:T(8,128)(2,1)} %param.15) | copy-start | bytes 1572868
  318.1 28.0 %all-gather.5.cloned.1.call-start = ((), (), s32[]{:S(2)}) async-start(), calls=%async_computation.9 | async-start | bytes 1310720 | tf_op jit(solution)/shard_map/all_gather | solution.py:197
  318.4 29.8 %copy-start.8 = (f32[16,32,2,128]{3,1,2,0:T(8,128)S(1)}, f32[16,32,2,128]{3,1,2,0:T(8,128)}, u32[]{:S(2)}) copy-start(f32[16,32,2,128]{3,1,2,0:T(8,128)} %copy-done.7) | copy-start | bytes 1572868
  318.4 29.8 %copy-start.10 = (f32[16,32,2,128]{3,2,1,0:T(2,128)S(1)}, f32[16,32,2,128]{3,2,1,0:T(2,128)}, u32[]{:S(2)}) copy-start(f32[16,32,2,128]{3,2,1,0:T(2,128)} %copy-done.9) | copy-start | bytes 1572868
  318.4 29.8 %copy-start.24 = (f32[16,32,2]{1,2,0:T(2,128)S(1)}, f32[16,32,2]{1,2,0:T(2,128)}, u32[]{:S(2)}) copy-start(f32[16,32,2]{1,2,0:T(2,128)} %get-tuple-element.29) | copy-start | bytes 12292
  319.3 249.7 %all-reduce.7.cloned.1.call-start = ((), (), s32[]{:S(2)}) async-start(), calls=%async_computation.11 | async-start | bytes 8388608
  353.5 2.9 copy-start.12
  353.5 2.9 copy-start.43
  353.5 2.9 copy-start.45
  397.8 172.7 %all-to-all-start.6 = ((bf16[64,4,6,1024]{3,0,2,1:T(8,128)(2,1)}), bf16[64,4,6,1024]{3,0,2,1:T(8,128)(2,1)S(1)}, u32[]{:S(2)}, u32[]{:S(2)}) async-start(bf16[64,4,6,1024]{3,0,2,1:T(8,128)(2,1)} %copy.134), calls=%async_computation.7 | async-start | bytes 6291456 | tf_op jit(solution)/shard_map/all_to_all | solution.py:179
  403.0 2.9 copy-start.47
  403.0 309.5 %reduce-scatter.2.cloned.1.call-start = ((), (), s32[]{:S(2)}) async-start(), calls=%async_computation.10 | async-start | bytes 1064960 | tf_op jit(solution)/shard_map/reduce_scatter | solution.py:214
  575.6 136.8 %copy-start.1 = (bf16[4,1024,256]{2,1,0:T(8,128)(2,1)S(1)}, bf16[4,1024,256]{2,1,0:T(8,128)(2,1)}, u32[]{:S(2)}) copy-start(bf16[4,1024,256]{2,1,0:T(8,128)(2,1)} %param.14) | copy-start | bytes 6291460
  (16 other events, 23.3 us)
Sparse Core Ops, SparseCore 0:
  61.1 24.8 all-gather.2
  320.8 25.3 all-gather.4
  368.0 200.9 all-reduce.6
  573.4 139.0 reduce-scatter.1
